TPU v7x, 256 devices: a whole 4x4x8 slice. The times are simulated.
256 devices in a mesh: row: 16 (over z, core), col: 16 (over y, x).
Axes of the slice: x: 4, y: 4, z: 8, core: 2. Of those that a mesh axis runs over, the one named last changes fastest.
Arguments:
- sigma_anc: float32 [48, 48, 128, 128], P('row', 'col'), as said below
- factor: float32 [16, 256, 128, 128], P('row', 'col'), may hold values from -1.25 to 1.25
- diag_inv: float32 [256, 128, 128], P('col'), as said below
- struct: int32 [256, 16], P('col'), may hold values from 0 to 47, all different within a row
Outputs:
- z_off: float32 [256, 48, 128, 128], P('col', 'row')
- z_diag: float32 [256, 128, 128], P(('col', 'row'))
Inputs may be any that keep to these rules, and one draw needn't show every extreme that they name: Each row of struct names 16 different ancestor blocks, and every ancestor block is named by some row. sigma_anc is symmetric: block [b, a] is the transpose of block [a, b]. Each diag_inv[k] is lower triangular with a positive diagonal.
All inputs are finite; a program needn't handle non-finite values.
Results may differ from a plain program's by a relative error of at most 0.0003.
Values sent between devices are 32-bit elements; how exact they have to be, the bound alone decides.
A program may use at most 128 MiB of HBM per device.

v0:
```python
import jax
import jax.numpy as jnp
from jax import lax
from jax.sharding import PartitionSpec as P

highest = lax.Precision.HIGHEST


def select_blocks(sigma_rows, slot_ids):
    return jnp.take(sigma_rows, slot_ids, axis=1)


def body(sigma_anc, factor, diag_inv, struct):
    row_count = sigma_anc.shape[0]
    node_count = diag_inv.shape[0]
    width = diag_inv.shape[1]
    row_index = lax.axis_index("row")
    own_rows = row_index * row_count + jnp.arange(row_count, dtype=jnp.int32)
    sigma_rows = lax.all_gather(sigma_anc, "col", axis=1, tiled=True)
    u_local = jnp.einsum("skij,kjl->skil", factor, diag_inv, precision=highest)
    empty = jnp.zeros((node_count, row_count, width, width), jnp.float32)

    def one_slot(running, element):
        u_slot, id_slot = element
        y_sum, u_rows = running
        picked = select_blocks(sigma_rows, id_slot)
        y_sum = y_sum + jnp.einsum("akij,kjl->kail", picked, u_slot, precision=highest)
        match = (id_slot[:, None] == own_rows[None, :]).astype(jnp.float32)
        u_rows = u_rows + match[:, :, None, None] * u_slot[:, None, :, :]
        return ((y_sum, u_rows), None)

    result, unused_out = lax.scan(
        one_slot,
        (empty, empty),
        (lax.all_gather(u_local, "row", axis=0, tiled=True), jnp.transpose(struct)),
    )
    y_rows, u_rows = result
    member = jnp.any(struct[:, :, None] == own_rows[None, None, :], axis=1)
    z_off = jnp.where(member[:, :, None, None], -y_rows, 0.0)
    partial_sum = jnp.einsum("kaij,kail->kjl", u_rows, y_rows, precision=highest)
    share_count = node_count // lax.axis_size("row")
    start_node = row_index * share_count
    inverse_share = lax.dynamic_slice_in_dim(diag_inv, start_node, share_count, 0)
    inverse_part = jnp.einsum("kij,kil->kjl", inverse_share, inverse_share, precision=highest)
    summed = lax.psum(partial_sum, "row")
    mine = lax.dynamic_slice_in_dim(summed, start_node, share_count, 0)
    return (z_off, inverse_part + mine)


def solution(mesh):
    in_specs = (
        P("row", "col", None, None),
        P("row", "col", None, None),
        P("col", None, None),
        P("col", None),
    )
    out_specs = (P("col", "row", None, None), P(("col", "row"), None, None))
    return jax.shard_map(body, mesh=mesh, in_specs=in_specs, out_specs=out_specs, check_vma=False)
```

profile of v0, /device:TPU:1, one launch (start us, length us, event | category | flops | bytes accessed | tf_op | source)
XLA Modules:
  0.0 607.2 jit_solution(9201970120801829042)
XLA Ops:
  13.0 82.0 %all-gather.3.cloned.1.call-done = f32[3,48,128,128]{3,2,1,0:T(8,128)} async-done(((f32[3,3,128,128]{3,2,1,0:T(8,128)}), f32[3,48,128,128]{3,2,1,0:T(8,128)}) %all-gather.3.cloned.1.call-update) | async-done | bytes 9437200 | tf_op jit(solution)/shard_map/all_gather | solution.py:19
  95.0 97.4 %all-gather.5.cloned.1.call-done = f32[16,16,128,128]{3,2,1,0:T(8,128)} async-done(((f32[1,16,128,128]{3,2,1,0:T(8,128)}), f32[16,16,128,128]{3,2,1,0:T(8,128)}) %all-gather.5.cloned.1.call-update) | async-done | bytes 16777232 | tf_op jit(solution)/shard_map/all_gather | solution.py:35
  192.4 287.7 %while.13 = (s32[]{:T(128)}, f32[16,3,128,128]{3,2,1,0:T(8,128)}, f32[16,3,128,128]{3,2,1,0:T(8,128)}, s32[16,16]{1,0:T(8,128)S(1)}, f32[3,48,128,128]{3,2,1,0:T...) while((s32[]{:T(128)}, f32[16,3,128,128]{3,2,1,0:T(8,128)}, ...), condition=%wide.region_2.3_spmd.clone, body=%wide.region_1.2_spmd.clone.sunk | while | flops 1212679424 | bytes 26220016 | solution.py:32
  192.5 6.1 gather_fusion
  198.5 6.2 %select_add_fusion.4 = f32[16,3,128,128]{3,2,1,0:T(8,128)} fusion(f32[16,3,128,128]{3,2,1,0:T(8,128)} %get-tuple-element.149, f32[16,3,128,128]{3,2,1,0:T(8,128)} %gather_fusion, pred[16]{0:T(512)(128)(4,1)S(1)} %get-tuple-element.137, pred[]{:T(512)S(6)} %compare.3, f32[16,16,128,128]{3,2,1,0:T(8,128)} %get-tuple-element.162, s32[]{:T(128)} %get-tuple-element.148), kind=kOutput, calls=%fused_computation.5.clone.1 | convolution fusion | flops 1210318848 | bytes 10486289 | tf_op jit(solution)/shard_map/while/body/eval_jaxpr/akij,kjl->kail/dot_general | solution.py:27
  208.2 6.1 gather_fusion
  214.3 6.7 %select_add_fusion.4 = f32[16,3,128,128]{3,2,1,0:T(8,128)} fusion(f32[16,3,128,128]{3,2,1,0:T(8,128)} %get-tuple-element.149, f32[16,3,128,128]{3,2,1,0:T(8,128)} %gather_fusion, pred[16]{0:T(512)(128)(4,1)S(1)} %get-tuple-element.137, pred[]{:T(512)S(6)} %compare.3, f32[16,16,128,128]{3,2,1,0:T(8,128)} %get-tuple-element.162, s32[]{:T(128)} %get-tuple-element.148), kind=kOutput, calls=%fused_computation.5.clone.1 | convolution fusion | flops 1210318848 | bytes 10486289 | tf_op jit(solution)/shard_map/while/body/eval_jaxpr/akij,kjl->kail/dot_general | solution.py:27
  226.4 6.1 gather_fusion
  232.4 6.7 %select_add_fusion.4 = f32[16,3,128,128]{3,2,1,0:T(8,128)} fusion(f32[16,3,128,128]{3,2,1,0:T(8,128)} %get-tuple-element.149, f32[16,3,128,128]{3,2,1,0:T(8,128)} %gather_fusion, pred[16]{0:T(512)(128)(4,1)S(1)} %get-tuple-element.137, pred[]{:T(512)S(6)} %compare.3, f32[16,16,128,128]{3,2,1,0:T(8,128)} %get-tuple-element.162, s32[]{:T(128)} %get-tuple-element.148), kind=kOutput, calls=%fused_computation.5.clone.1 | convolution fusion | flops 1210318848 | bytes 10486289 | tf_op jit(solution)/shard_map/while/body/eval_jaxpr/akij,kjl->kail/dot_general | solution.py:27
  244.5 6.1 gather_fusion
  250.6 6.7 %select_add_fusion.4 = f32[16,3,128,128]{3,2,1,0:T(8,128)} fusion(f32[16,3,128,128]{3,2,1,0:T(8,128)} %get-tuple-element.149, f32[16,3,128,128]{3,2,1,0:T(8,128)} %gather_fusion, pred[16]{0:T(512)(128)(4,1)S(1)} %get-tuple-element.137, pred[]{:T(512)S(6)} %compare.3, f32[16,16,128,128]{3,2,1,0:T(8,128)} %get-tuple-element.162, s32[]{:T(128)} %get-tuple-element.148), kind=kOutput, calls=%fused_computation.5.clone.1 | convolution fusion | flops 1210318848 | bytes 10486289 | tf_op jit(solution)/shard_map/while/body/eval_jaxpr/akij,kjl->kail/dot_general | solution.py:27
  262.6 6.1 gather_fusion
  268.7 6.7 %select_add_fusion.4 = f32[16,3,128,128]{3,2,1,0:T(8,128)} fusion(f32[16,3,128,128]{3,2,1,0:T(8,128)} %get-tuple-element.149, f32[16,3,128,128]{3,2,1,0:T(8,128)} %gather_fusion, pred[16]{0:T(512)(128)(4,1)S(1)} %get-tuple-element.137, pred[]{:T(512)S(6)} %compare.3, f32[16,16,128,128]{3,2,1,0:T(8,128)} %get-tuple-element.162, s32[]{:T(128)} %get-tuple-element.148), kind=kOutput, calls=%fused_computation.5.clone.1 | convolution fusion | flops 1210318848 | bytes 10486289 | tf_op jit(solution)/shard_map/while/body/eval_jaxpr/akij,kjl->kail/dot_general | solution.py:27
  280.7 6.1 gather_fusion
  286.8 6.7 %select_add_fusion.4 = f32[16,3,128,128]{3,2,1,0:T(8,128)} fusion(f32[16,3,128,128]{3,2,1,0:T(8,128)} %get-tuple-element.149, f32[16,3,128,128]{3,2,1,0:T(8,128)} %gather_fusion, pred[16]{0:T(512)(128)(4,1)S(1)} %get-tuple-element.137, pred[]{:T(512)S(6)} %compare.3, f32[16,16,128,128]{3,2,1,0:T(8,128)} %get-tuple-element.162, s32[]{:T(128)} %get-tuple-element.148), kind=kOutput, calls=%fused_computation.5.clone.1 | convolution fusion | flops 1210318848 | bytes 10486289 | tf_op jit(solution)/shard_map/while/body/eval_jaxpr/akij,kjl->kail/dot_general | solution.py:27
  298.9 6.1 gather_fusion
  305.0 6.7 %select_add_fusion.4 = f32[16,3,128,128]{3,2,1,0:T(8,128)} fusion(f32[16,3,128,128]{3,2,1,0:T(8,128)} %get-tuple-element.149, f32[16,3,128,128]{3,2,1,0:T(8,128)} %gather_fusion, pred[16]{0:T(512)(128)(4,1)S(1)} %get-tuple-element.137, pred[]{:T(512)S(6)} %compare.3, f32[16,16,128,128]{3,2,1,0:T(8,128)} %get-tuple-element.162, s32[]{:T(128)} %get-tuple-element.148), kind=kOutput, calls=%fused_computation.5.clone.1 | convolution fusion | flops 1210318848 | bytes 10486289 | tf_op jit(solution)/shard_map/while/body/eval_jaxpr/akij,kjl->kail/dot_general | solution.py:27
  317.0 6.1 gather_fusion
  323.1 6.7 %select_add_fusion.4 = f32[16,3,128,128]{3,2,1,0:T(8,128)} fusion(f32[16,3,128,128]{3,2,1,0:T(8,128)} %get-tuple-element.149, f32[16,3,128,128]{3,2,1,0:T(8,128)} %gather_fusion, pred[16]{0:T(512)(128)(4,1)S(1)} %get-tuple-element.137, pred[]{:T(512)S(6)} %compare.3, f32[16,16,128,128]{3,2,1,0:T(8,128)} %get-tuple-element.162, s32[]{:T(128)} %get-tuple-element.148), kind=kOutput, calls=%fused_computation.5.clone.1 | convolution fusion | flops 1210318848 | bytes 10486289 | tf_op jit(solution)/shard_map/while/body/eval_jaxpr/akij,kjl->kail/dot_general | solution.py:27
  335.1 6.1 gather_fusion
  341.2 6.7 %select_add_fusion.4 = f32[16,3,128,128]{3,2,1,0:T(8,128)} fusion(f32[16,3,128,128]{3,2,1,0:T(8,128)} %get-tuple-element.149, f32[16,3,128,128]{3,2,1,0:T(8,128)} %gather_fusion, pred[16]{0:T(512)(128)(4,1)S(1)} %get-tuple-element.137, pred[]{:T(512)S(6)} %compare.3, f32[16,16,128,128]{3,2,1,0:T(8,128)} %get-tuple-element.162, s32[]{:T(128)} %get-tuple-element.148), kind=kOutput, calls=%fused_computation.5.clone.1 | convolution fusion | flops 1210318848 | bytes 10486289 | tf_op jit(solution)/shard_map/while/body/eval_jaxpr/akij,kjl->kail/dot_general | solution.py:27
  353.3 6.1 gather_fusion
  359.4 6.7 %select_add_fusion.4 = f32[16,3,128,128]{3,2,1,0:T(8,128)} fusion(f32[16,3,128,128]{3,2,1,0:T(8,128)} %get-tuple-element.149, f32[16,3,128,128]{3,2,1,0:T(8,128)} %gather_fusion, pred[16]{0:T(512)(128)(4,1)S(1)} %get-tuple-element.137, pred[]{:T(512)S(6)} %compare.3, f32[16,16,128,128]{3,2,1,0:T(8,128)} %get-tuple-element.162, s32[]{:T(128)} %get-tuple-element.148), kind=kOutput, calls=%fused_computation.5.clone.1 | convolution fusion | flops 1210318848 | bytes 10486289 | tf_op jit(solution)/shard_map/while/body/eval_jaxpr/akij,kjl->kail/dot_general | solution.py:27
  371.4 6.1 gather_fusion
  377.5 6.7 %select_add_fusion.4 = f32[16,3,128,128]{3,2,1,0:T(8,128)} fusion(f32[16,3,128,128]{3,2,1,0:T(8,128)} %get-tuple-element.149, f32[16,3,128,128]{3,2,1,0:T(8,128)} %gather_fusion, pred[16]{0:T(512)(128)(4,1)S(1)} %get-tuple-element.137, pred[]{:T(512)S(6)} %compare.3, f32[16,16,128,128]{3,2,1,0:T(8,128)} %get-tuple-element.162, s32[]{:T(128)} %get-tuple-element.148), kind=kOutput, calls=%fused_computation.5.clone.1 | convolution fusion | flops 1210318848 | bytes 10486289 | tf_op jit(solution)/shard_map/while/body/eval_jaxpr/akij,kjl->kail/dot_general | solution.py:27
  395.6 6.7 %select_add_fusion.4 = f32[16,3,128,128]{3,2,1,0:T(8,128)} fusion(f32[16,3,128,128]{3,2,1,0:T(8,128)} %get-tuple-element.149, f32[16,3,128,128]{3,2,1,0:T(8,128)} %gather_fusion, pred[16]{0:T(512)(128)(4,1)S(1)} %get-tuple-element.137, pred[]{:T(512)S(6)} %compare.3, f32[16,16,128,128]{3,2,1,0:T(8,128)} %get-tuple-element.162, s32[]{:T(128)} %get-tuple-element.148), kind=kOutput, calls=%fused_computation.5.clone.1 | convolution fusion | flops 1210318848 | bytes 10486289 | tf_op jit(solution)/shard_map/while/body/eval_jaxpr/akij,kjl->kail/dot_general | solution.py:27
  413.8 6.7 %select_add_fusion.4 = f32[16,3,128,128]{3,2,1,0:T(8,128)} fusion(f32[16,3,128,128]{3,2,1,0:T(8,128)} %get-tuple-element.149, f32[16,3,128,128]{3,2,1,0:T(8,128)} %gather_fusion, pred[16]{0:T(512)(128)(4,1)S(1)} %get-tuple-element.137, pred[]{:T(512)S(6)} %compare.3, f32[16,16,128,128]{3,2,1,0:T(8,128)} %get-tuple-element.162, s32[]{:T(128)} %get-tuple-element.148), kind=kOutput, calls=%fused_computation.5.clone.1 | convolution fusion | flops 1210318848 | bytes 10486289 | tf_op jit(solution)/shard_map/while/body/eval_jaxpr/akij,kjl->kail/dot_general | solution.py:27
  431.9 6.7 %select_add_fusion.4 = f32[16,3,128,128]{3,2,1,0:T(8,128)} fusion(f32[16,3,128,128]{3,2,1,0:T(8,128)} %get-tuple-element.149, f32[16,3,128,128]{3,2,1,0:T(8,128)} %gather_fusion, pred[16]{0:T(512)(128)(4,1)S(1)} %get-tuple-element.137, pred[]{:T(512)S(6)} %compare.3, f32[16,16,128,128]{3,2,1,0:T(8,128)} %get-tuple-element.162, s32[]{:T(128)} %get-tuple-element.148), kind=kOutput, calls=%fused_computation.5.clone.1 | convolution fusion | flops 1210318848 | bytes 10486289 | tf_op jit(solution)/shard_map/while/body/eval_jaxpr/akij,kjl->kail/dot_general | solution.py:27
  450.0 6.7 %select_add_fusion.4 = f32[16,3,128,128]{3,2,1,0:T(8,128)} fusion(f32[16,3,128,128]{3,2,1,0:T(8,128)} %get-tuple-element.149, f32[16,3,128,128]{3,2,1,0:T(8,128)} %gather_fusion, pred[16]{0:T(512)(128)(4,1)S(1)} %get-tuple-element.137, pred[]{:T(512)S(6)} %compare.3, f32[16,16,128,128]{3,2,1,0:T(8,128)} %get-tuple-element.162, s32[]{:T(128)} %get-tuple-element.148), kind=kOutput, calls=%fused_computation.5.clone.1 | convolution fusion | flops 1210318848 | bytes 10486289 | tf_op jit(solution)/shard_map/while/body/eval_jaxpr/akij,kjl->kail/dot_general | solution.py:27
  468.2 6.7 %select_add_fusion.4 = f32[16,3,128,128]{3,2,1,0:T(8,128)} fusion(f32[16,3,128,128]{3,2,1,0:T(8,128)} %get-tuple-element.149, f32[16,3,128,128]{3,2,1,0:T(8,128)} %gather_fusion, pred[16]{0:T(512)(128)(4,1)S(1)} %get-tuple-element.137, pred[]{:T(512)S(6)} %compare.3, f32[16,16,128,128]{3,2,1,0:T(8,128)} %get-tuple-element.162, s32[]{:T(128)} %get-tuple-element.148), kind=kOutput, calls=%fused_computation.5.clone.1 | convolution fusion | flops 1210318848 | bytes 10486289 | tf_op jit(solution)/shard_map/while/body/eval_jaxpr/akij,kjl->kail/dot_general | solution.py:27
  480.2 9.0 %convolution_bitcast_fusion = f32[16,128,128]{2,1,0:T(8,128)} fusion(f32[16,3,128,128]{3,2,1,0:T(8,128)} %get-tuple-element.41, f32[16,3,128,128]{3,2,1,0:T(8,128)} %get-tuple-element.40), kind=kOutput, calls=%fused_computation.24 | convolution fusion | flops 1207959552 | bytes 7340032 | tf_op jit(solution)/shard_map/kaij,kail->kjl/dot_general | solution.py:40
  493.4 105.4 %all-reduce.2.cloned.1.call-done = f32[16,128,128]{2,1,0:T(8,128)} async-done(((f32[16,128,128]{2,1,0:T(8,128)}), f32[16,128,128]{2,1,0:T(8,128)}) %all-reduce.2.cloned.1.call-update) | async-done | bytes 1048592 | tf_op jit(solution)/shard_map/psum | solution.py:45
  (137 shorter events, 126.0 us)
Async XLA Ops:
  7.2 1.2 copy-start
  7.2 87.8 %all-gather.3.cloned.1.call-start = ((), (), s32[]{:S(2)}) async-start(), calls=%async_computation | async-start | bytes 10027008 | tf_op jit(solution)/shard_map/all_gather | solution.py:19
  7.9 5.0 copy-start.1
  7.9 184.5 %all-gather.5.cloned.1.call-start = ((), (), s32[]{:S(2)}) async-start(), calls=%async_computation.1 | async-start | bytes 17825792 | tf_op jit(solution)/shard_map/all_gather | solution.py:35
  12.8 586.0 %all-reduce.2.cloned.1.call-start = ((), (), s32[]{:S(2)}) async-start(), calls=%async_computation.2 | async-start | bytes 2097152 | tf_op jit(solution)/shard_map/psum | solution.py:45
Sparse Core Ops, SparseCore 0:
  10.4 84.5 all-gather.2
  96.8 95.5 all-gather.4
  489.3 109.5 all-reduce.1
where the time goes:
time: 609 us; the launch traced here: 607 us
  waiting for transfers between devices  286 us (47%)
  local copies, waits for them, and re-layouts  120 us (20%)
  matrix products  120 us (20%)
  other arithmetic  67.3 us (11%)
  between operations  13.8 us (2%)
    dot_general x16, matrix products, one_slot(): jnp.einsum('akij,kjl->kail', picked, u_slot, precision=highest)  106 us
    psum x1, waiting for transfers between devices, body(): summed = lax.psum(partial_sum, 'row')  105 us
    all_gather x1, waiting for transfers between devices, body(): lax.all_gather(u_local, 'row', axis=0, tiled=True)  97.4 us
    gather x16, local copies, waits for them, and re-layouts, select_blocks(): return jnp.take(sigma_rows, slot_ids, axis=1)  97.1 us
    all_gather x1, waiting for transfers between devices, body(): sigma_rows = lax.all_gather(sigma_anc, 'col', axis=1, tiled=True)  82 us
    add x16, other arithmetic, one_slot(): u_rows = u_rows + match[:, :, None, None] * u_slot[:, None, :, :]  61.5 us
    squeeze x16, local copies, waits for them, and re-layouts, body(): lax.scan(one_slot, (empty, empty), (lax.all_gather(u_local, 'row', axis=0...  20.7 us
  transfers between devices with their start and end apart: 3, of which 3 were waited for; matrix products, arithmetic and copies ran while one was open for 1% of the time, Pallas kernels for 0%

commit v1 on v0

--- a/solution.py
+++ b/solution.py
@@ -32,7 +32,12 @@
     result, unused_out = lax.scan(
         one_slot,
         (empty, empty),
-        (lax.all_gather(u_local, "row", axis=0, tiled=True), jnp.transpose(struct)),
+        (
+            jnp.concatenate(
+                lax.all_to_all(jnp.stack([u_local] * lax.axis_size("row")), "row", 0, 0), axis=0
+            ),
+            jnp.transpose(struct),
+        ),
     )
     y_rows, u_rows = result
     member = jnp.any(struct[:, :, None] == own_rows[None, None, :], axis=1)

time: 609 us -> 812 us (1.33)
  waiting for transfers between devices: 286 us -> 470 us
  starting transfers between devices: 0.12 us -> 10.4 us
    all_to_all x0 -> x1, waiting for transfers between devices: none -> 278 us  [body(): lax.all_to_all(jnp.stack([u_local] * lax.axis_size('row')), 'row', 0, 0)]
    all_gather x1 -> x0, waiting for transfers between devices: 97.4 us -> none  [body(): lax.all_gather(u_local, 'row', axis=0, tiled=True)]
    all_to_all x0 -> x1, starting transfers between devices: none -> 10.1 us  [body(): lax.all_to_all(jnp.stack([u_local] * lax.axis_size('row')), 'row', 0, 0)]
where the time goes in v1:
time: 812 us; the launch traced here: 810 us
  waiting for transfers between devices  470 us (58%)
  local copies, waits for them, and re-layouts  128 us (16%)
  matrix products  120 us (15%)
  other arithmetic  66.8 us (8%)
  between operations  14.1 us (2%)
  starting transfers between devices  10.4 us (1%)
    all_to_all x1, waiting for transfers between devices, body(): lax.all_to_all(jnp.stack([u_local] * lax.axis_size('row')), 'row', 0, 0)  278 us
    psum x1, waiting for transfers between devices, body(): summed = lax.psum(partial_sum, 'row')  107 us
    dot_general x16, matrix products, one_slot(): jnp.einsum('akij,kjl->kail', picked, u_slot, precision=highest)  106 us
    gather x16, local copies, waits for them, and re-layouts, select_blocks(): return jnp.take(sigma_rows, slot_ids, axis=1)  97.2 us
    all_gather x1, waiting for transfers between devices, body(): sigma_rows = lax.all_gather(sigma_anc, 'col', axis=1, tiled=True)  84 us
    add x16, other arithmetic, one_slot(): u_rows = u_rows + match[:, :, None, None] * u_slot[:, None, :, :]  61.1 us
    squeeze x16, local copies, waits for them, and re-layouts, body(): lax.scan(one_slot, (empty, empty), (jnp.concatenate(lax.all_to_all(jnp.st...  20.7 us
  transfers between devices with their start and end apart: 3, of which 3 were waited for; matrix products, arithmetic and copies ran while one was open for 1% of the time, Pallas kernels for 0%

profile of v1, /device:TPU:1, one launch (start us, length us, event | category | flops | bytes accessed | tf_op | source)
XLA Modules:
  0.0 809.7 jit_solution(4318364873117433492)
XLA Ops:
  11.8 7.9 stack.2
  19.7 10.1 %all-to-all-start = ((f32[16,1,16,128,128]{4,3,2,1,0:T(8,128)}), f32[16,1,16,128,128]{4,3,2,1,0:T(8,128)}, u32[]{:S(2)}, u32[]{:S(2)}) async-start(f32[16,1,16,128,128]{4,3,2,1,0:T(8,128)} %stack.2), calls=%async_computation | async-start | bytes 33554432 | tf_op jit(solution)/shard_map/all_to_all | solution.py:37
  30.9 84.0 %all-gather.2.cloned.1.call-done = f32[3,48,128,128]{3,2,1,0:T(8,128)} async-done(((f32[3,3,128,128]{3,2,1,0:T(8,128)}), f32[3,48,128,128]{3,2,1,0:T(8,128)}) %all-gather.2.cloned.1.call-update) | async-done | bytes 9437200 | tf_op jit(solution)/shard_map/all_gather | solution.py:19
  114.9 278.2 %all-to-all-done = f32[16,1,16,128,128]{4,3,2,1,0:T(8,128)} async-done(((f32[16,1,16,128,128]{4,3,2,1,0:T(8,128)}), f32[16,1,16,128,128]{4,3,2,1,0:T(8,128)}, u32[]{:S(2)}, u32[]{:S(2)}) %all-to-all-start) | async-done | bytes 16777248 | tf_op jit(solution)/shard_map/all_to_all | solution.py:37
  393.1 287.4 %while.13 = (s32[]{:T(128)}, f32[16,3,128,128]{3,2,1,0:T(8,128)}, f32[16,3,128,128]{3,2,1,0:T(8,128)}, s32[16,16]{1,0:T(8,128)S(1)}, f32[3,48,128,128]{3,2,1,0:T...) while((s32[]{:T(128)}, f32[16,3,128,128]{3,2,1,0:T(8,128)}, ...), condition=%wide.region_2.3_spmd.clone, body=%wide.region_1.2_spmd.clone.sunk | while | flops 1212679424 | bytes 26220016 | solution.py:32
  393.1 6.1 gather_fusion
  399.2 6.2 select_add_fusion.4
  408.9 6.1 gather_fusion
  415.0 6.7 select_add_fusion.4
  433.1 6.7 select_add_fusion.4
  451.2 6.7 select_add_fusion.4
  469.3 6.7 select_add_fusion.4
  487.4 6.7 select_add_fusion.4
  505.5 6.7 select_add_fusion.4
  517.5 6.1 gather_fusion
  523.6 6.7 select_add_fusion.4
  535.6 6.1 gather_fusion
  541.7 6.7 select_add_fusion.4
  559.8 6.7 select_add_fusion.4
  571.9 6.1 gather_fusion
  578.0 6.7 select_add_fusion.4
  590.0 6.1 gather_fusion
  596.1 6.7 select_add_fusion.4
  614.2 6.7 select_add_fusion.4
  626.2 6.1 gather_fusion
  632.3 6.7 select_add_fusion.4
  644.3 6.1 gather_fusion
  650.4 6.7 select_add_fusion.4
  662.4 6.1 gather_fusion
  668.5 6.7 select_add_fusion.4
  680.5 9.0 %convolution_bitcast_fusion = f32[16,128,128]{2,1,0:T(8,128)} fusion(f32[16,3,128,128]{3,2,1,0:T(8,128)} %get-tuple-element.41, f32[16,3,128,128]{3,2,1,0:T(8,128)} %get-tuple-element.40), kind=kOutput, calls=%fused_computation.24 | convolution fusion | flops 1207959552 | bytes 7340032 | tf_op jit(solution)/shard_map/kaij,kail->kjl/dot_general | solution.py:45
  693.8 107.3 %all-reduce.2.cloned.1.call-done = f32[16,128,128]{2,1,0:T(8,128)} async-done(((f32[16,128,128]{2,1,0:T(8,128)}), f32[16,128,128]{2,1,0:T(8,128)}) %all-reduce.2.cloned.1.call-update) | async-done | bytes 1048592 | tf_op jit(solution)/shard_map/psum | solution.py:50
  (137 shorter events, 137.6 us)
Async XLA Ops:
  7.2 1.2 copy-start
  19.7 11.1 %copy-start.1 = (s32[16,16]{1,0:T(8,128)S(1)}, s32[16,16]{1,0:T(8,128)}, u32[]{:S(2)}) copy-start(s32[16,16]{1,0:T(8,128)} %param.9) | copy-start | bytes 3076
  19.7 373.4 %all-to-all-start = ((f32[16,1,16,128,128]{4,3,2,1,0:T(8,128)}), f32[16,1,16,128,128]{4,3,2,1,0:T(8,128)}, u32[]{:S(2)}, u32[]{:S(2)}) async-start(f32[16,1,16,128,128]{4,3,2,1,0:T(8,128)} %stack.2), calls=%async_computation | async-start | bytes 33554432 | tf_op jit(solution)/shard_map/all_to_all | solution.py:37
  29.9 85.1 %all-gather.2.cloned.1.call-start = ((), (), s32[]{:S(2)}) async-start(), calls=%async_computation.1 | async-start | bytes 10027008 | tf_op jit(solution)/shard_map/all_gather | solution.py:19
  30.6 770.5 %all-reduce.2.cloned.1.call-start = ((), (), s32[]{:S(2)}) async-start(), calls=%async_computation.2 | async-start | bytes 2097152 | tf_op jit(solution)/shard_map/psum | solution.py:50
Sparse Core Ops, SparseCore 0:
  33.1 81.7 all-gather.1
  689.6 111.3 all-reduce.1
